TPU v7x, 32 devices: a whole 2x2x4 slice. The times are simulated.
32 devices in a mesh: lon: 8 (over y, x, core), lev: 4 (over z).
Axes of the slice: x: 2, y: 2, z: 4, core: 2. Of those that a mesh axis runs over, the one named last changes fastest.
Arguments:
- tracers: float32 [32, 16, 64, 1024], P(None, 'lev', None, 'lon'), may hold values from 0.1 to 10
- offsets: int32 [64], replicated, may hold values from 0 to 1023
- fraction: float32 [64], replicated, may hold values from 0 to 1
- bin_class: int32 [8], replicated, may hold values from 0 to 7
- thickness: float32 [16], P('lev'), may hold values from 0.5 to 2
Outputs:
- settled: float32 [32, 16, 64, 1024], P(None, 'lev', None, 'lon')
All inputs are finite; a program needn't handle non-finite values.
Results may differ from a plain program's by a relative error of at most 0.00002.
Values sent between devices are 32-bit elements; how exact they have to be, the bound alone decides.
A program may use at most 128 MiB of HBM per device.

v0:
```python
import jax
import jax.numpy as jnp
from jax import lax
from jax.sharding import PartitionSpec as P

GROUPS = 4


def passed_along(value, axis, steps):
    count = lax.axis_size(axis)
    pairs = [(source, (source + steps) % count) for source in range(count)]
    return lax.ppermute(value, axis, pairs)


def from_behind(value, axis, by):
    count = lax.axis_size(axis)
    pairs = [(i, i + by) for i in range(count) if 0 <= i + by < count]
    return lax.ppermute(value, axis, pairs)


def roll_rows(field, amount, limit):
    steps = max(1, (limit - 1).bit_length())
    for bit in range(steps):
        chosen = (amount // (1 << bit) % 2 == 1)[:, None]
        field = jnp.where(chosen, jnp.roll(field, 1 << bit, axis=-1), field)
    return field


def on_device(tracers, offsets, fraction, bin_class, thickness):
    width = tracers.shape[-1]
    devices = lax.axis_size("lon")
    share = fraction[:, None]
    quotient = offsets // width
    remainder = offsets % width
    block = tracers
    for bit in range((devices - 1).bit_length()):
        arrived = passed_along(block, "lon", 1 << bit)
        taken = quotient // (1 << bit) % 2 == 1
        block = jnp.where(taken[:, None], arrived, block)
    upstream = passed_along(block, "lon", 1)
    joined = jnp.concatenate([upstream, block], axis=-1)
    rolled = roll_rows(joined, remainder, width)
    left_part = rolled[..., width:]
    right_part = rolled[..., width - 1 : 2 * width - 1]
    moved = (1.0 - share) * left_part + share * right_part
    levels = tracers.shape[1]
    speed = 0.5 * jnp.exp2(jnp.repeat(bin_class, GROUPS).astype(jnp.float32))
    ratio = speed[:, None] / thickness[None, :]

    def sweep(incoming):
        value = incoming
        columns = []
        for level in range(levels):
            rate = ratio[:, level][:, None, None]
            value = (moved[:, level] + rate * value) / (1.0 + rate)
            columns.append(value)
        return jnp.stack(columns, axis=1)

    zeros_start = jnp.zeros((moved.shape[0], moved.shape[2], moved.shape[3]), jnp.float32)
    bottom = sweep(zeros_start)[:, -1]
    factor = jnp.prod(ratio / (1.0 + ratio), axis=1)[:, None, None]
    incoming = zeros_start
    for step in range(lax.axis_size("lev") - 1):
        incoming = from_behind(factor * incoming + bottom, "lev", 1)
    return sweep(incoming)


def solution(mesh):
    in_specs = (P(None, "lev", None, "lon"), P(), P(), P(), P("lev"))
    out_specs = P(None, "lev", None, "lon")
    return jax.shard_map(
        on_device, mesh=mesh, in_specs=in_specs, out_specs=out_specs, check_vma=False
    )
```

profile of v0, /device:TPU:1, one launch (start us, length us, event | category | flops | bytes accessed | tf_op | source)
XLA Modules:
  0.0 401.3 jit_solution(7286082989974534394)
XLA Ops:
  0.0 2.7 copy.11
  2.7 2.7 collective-permute-start
  5.4 45.4 %collective-permute-done = f32[32,4,64,128]{3,2,0,1:T(8,128)S(1)} collective-permute-done((f32[32,4,64,128]{3,2,0,1:T(8,128)S(1)}, f32[32,4,64,128]{3,2,0,1:T(8,128)S(1)}, u32[]{:S(2)}, u32[]{:S(2)}) %collective-permute-start) | collective-permute-done | bytes 4194336 | tf_op jit(solution)/shard_map/ppermute | solution.py:12
  53.5 90.2 %collective-permute-done.1 = f32[32,4,64,128]{3,2,0,1:T(8,128)S(1)} collective-permute-done((f32[32,4,64,128]{3,2,0,1:T(8,128)S(1)}, f32[32,4,64,128]{3,2,0,1:T(8,128)S(1)}, u32[]{:S(2)}, u32[]{:S(2)}) %collective-permute-start.1) | collective-permute-done | bytes 4194336 | tf_op jit(solution)/shard_map/ppermute | solution.py:12
  145.6 89.1 %collective-permute-done.2 = f32[32,4,64,128]{3,2,0,1:T(8,128)S(1)} collective-permute-done((f32[32,4,64,128]{3,2,0,1:T(8,128)S(1)}, f32[32,4,64,128]{3,2,0,1:T(8,128)S(1)}, u32[]{:S(2)}, u32[]{:S(2)}) %collective-permute-start.2) | collective-permute-done | bytes 4194336 | tf_op jit(solution)/shard_map/ppermute | solution.py:12
  234.8 3.0 broadcast_select_fusion.2
  237.8 3.7 collective-permute-start.3
  241.8 3.3 slice.119
  245.2 42.1 %collective-permute-done.3 = f32[32,4,64,128]{3,2,0,1:T(8,128)} collective-permute-done((f32[32,4,64,128]{3,2,0,1:T(8,128)}, f32[32,4,64,128]{3,2,0,1:T(8,128)}, u32[]{:S(2)}, u32[]{:S(2)}) %collective-permute-start.3) | collective-permute-done | bytes 4194336 | tf_op jit(solution)/shard_map/ppermute | solution.py:12
  287.2 3.9 fusion
  291.1 5.0 %fusion.1 = f32[32,4,64,256]{3,2,0,1:T(8,128)S(1)} fusion(f32[32,4,64,128]{3,2,0,1:T(8,128)} %broadcast_select_fusion.2, f32[32,4,64,128]{3,2,0,1:T(8,128)} %collective-permute-done.3, f32[32,4,64,255]{3,2,0,1:T(8,128)S(1)} %fusion, f32[32,4,64,1]{3,2,0,1:T(8,128)S(1)} %slice.119, pred[64]{0:T(512)(128)(4,1)S(1)} %get-tuple-element.28), kind=kLoop, calls=%fused_computation.4 | loop fusion | flops 6291456 | bytes 25165888 | tf_op jit(solution)/shard_map/jit(_where)/select_n | solution.py:25
  297.2 2.9 maximum_select_fusion
  301.2 2.9 maximum_select_fusion.1
  305.3 2.9 maximum_select_fusion.2
  309.3 3.1 maximum_select_fusion.3
  313.5 2.9 maximum_select_fusion.4
  317.5 4.6 %maximum_select_fusion.5 = f32[32,4,64,256]{3,2,0,1:T(8,128)} fusion(f32[32,4,64,256]{3,2,0,1:T(8,128)S(1)} %maximum_select_fusion.4, f32[32,4,64,192]{3,2,0,1:T(8,128)S(1)} %bitcast.77, f32[32,4,64,64]{3,2,0,1:T(8,128)S(1)} %slice.132, pred[64]{0:T(512)(128)(4,1)S(1)} %get-tuple-element.9), kind=kLoop, calls=%fused_computation.10 | loop fusion | flops 4194304 | bytes 25165888 | tf_op jit(solution)/shard_map/jit(_where)/select_n | solution.py:25
  322.2 5.8 %fusion.2 = f32[32,4,64,128]{3,2,0,1:T(8,128)S(1)} fusion(f32[32,4,64,256]{3,2,0,1:T(8,128)} %maximum_select_fusion.5, f32[64]{0:T(128)S(1)} %copy-done.1, f32[64]{0:T(128)S(1)} %broadcast_subtract_fusion), kind=kLoop, calls=%fused_computation.12 | loop fusion | flops 3145728 | bytes 12583424 | tf_op jit(solution)/shard_map/add | solution.py:45
  328.6 3.3 collective-permute-start.4
  331.9 20.1 %collective-permute-done.4 = f32[32,64,128]{2,1,0:T(8,128)S(1)} collective-permute-done((f32[32,64,128]{2,1,0:T(8,128)S(1)}, f32[32,64,128]{2,1,0:T(8,128)S(1)}, u32[]{:S(2)}, u32[]{:S(2)}) %collective-permute-start.4) | collective-permute-done | bytes 1048608 | tf_op jit(solution)/shard_map/ppermute | solution.py:18
  352.2 4.2 %collective-permute-start.5 = (f32[32,64,128]{2,1,0:T(8,128)S(1)}, f32[32,64,128]{2,1,0:T(8,128)S(1)}, u32[]{:S(2)}, u32[]{:S(2)}) collective-permute-start(f32[32,64,128]{2,1,0:T(8,128)S(1)} %multiply_add_fusion.1), channel_id=1, source_target_pairs={{0,1},{1,2},{2,3},{4,5},{5,6},{6,7},{8,9},{9,10},{10,11},{12,13},{... | collective-permute-start | bytes 3145736 | tf_op jit(solution)/shard_map/ppermute | solution.py:18
  356.4 19.2 %collective-permute-done.5 = f32[32,64,128]{2,1,0:T(8,128)S(1)} collective-permute-done((f32[32,64,128]{2,1,0:T(8,128)S(1)}, f32[32,64,128]{2,1,0:T(8,128)S(1)}, u32[]{:S(2)}, u32[]{:S(2)}) %collective-permute-start.5) | collective-permute-done | bytes 1048608 | tf_op jit(solution)/shard_map/ppermute | solution.py:18
  375.7 4.2 %collective-permute-start.6 = (f32[32,64,128]{2,1,0:T(8,128)S(1)}, f32[32,64,128]{2,1,0:T(8,128)S(1)}, u32[]{:S(2)}, u32[]{:S(2)}) collective-permute-start(f32[32,64,128]{2,1,0:T(8,128)S(1)} %multiply_add_fusion), channel_id=1, source_target_pairs={{0,1},{1,2},{2,3},{4,5},{5,6},{6,7},{8,9},{9,10},{10,11},{12,13},{... | collective-permute-start | bytes 3145736 | tf_op jit(solution)/shard_map/ppermute | solution.py:18
  379.9 18.2 %collective-permute-done.6 = f32[32,64,128]{2,1,0:T(8,128)S(1)} collective-permute-done((f32[32,64,128]{2,1,0:T(8,128)S(1)}, f32[32,64,128]{2,1,0:T(8,128)S(1)}, u32[]{:S(2)}, u32[]{:S(2)}) %collective-permute-start.6) | collective-permute-done | bytes 1048608 | tf_op jit(solution)/shard_map/ppermute | solution.py:18
  (36 shorter events, 16.0 us)
Async XLA Ops:
  0.0 50.8 %copy-start = (f32[32,4,64,128]{3,2,1,0:T(8,128)S(1)}, f32[32,4,64,128]{3,2,1,0:T(8,128)}, u32[]{:S(2)}) copy-start(f32[32,4,64,128]{3,2,1,0:T(8,128)} %param.5) | copy-start | bytes 12582916
  0.0 5.3 %copy-start.2 = (s32[64]{0:T(128)S(1)}, s32[64]{0:T(128)}, u32[]{:S(2)}) copy-start(s32[64]{0:T(128)} %param.6) | copy-start | bytes 772
  2.7 48.1 %collective-permute-start = (f32[32,4,64,128]{3,2,0,1:T(8,128)S(1)}, f32[32,4,64,128]{3,2,0,1:T(8,128)S(1)}, u32[]{:S(2)}, u32[]{:S(2)}) collective-permute-start(f32[32,4,64,128]{3,2,0,1:T(8,128)S(1)} %copy.11), channel_id=1, source_target_pairs={{0,4},{4,8},{8,12},{12,16},{16,20},{20,24},{24,28},{28,0},{1,5},{5... | collective-permute-start | bytes 12582920 | tf_op jit(solution)/shard_map/ppermute | solution.py:12
  52.2 91.5 %collective-permute-start.1 = (f32[32,4,64,128]{3,2,0,1:T(8,128)S(1)}, f32[32,4,64,128]{3,2,0,1:T(8,128)S(1)}, u32[]{:S(2)}, u32[]{:S(2)}) collective-permute-start(f32[32,4,64,128]{3,2,0,1:T(8,128)S(1)} %broadcast_select_fusion), channel_id=1, source_target_pairs={{0,8},{4,12},{8,16},{12,20},{16,24},{20,28},{24,0},{28,4},{1,9},{5... | collective-permute-start | bytes 12582920 | tf_op jit(solution)/shard_map/ppermute | solution.py:12
  145.1 89.7 %collective-permute-start.2 = (f32[32,4,64,128]{3,2,0,1:T(8,128)S(1)}, f32[32,4,64,128]{3,2,0,1:T(8,128)S(1)}, u32[]{:S(2)}, u32[]{:S(2)}) collective-permute-start(f32[32,4,64,128]{3,2,0,1:T(8,128)S(1)} %broadcast_select_fusion.1), channel_id=1, source_target_pairs={{0,16},{4,20},{8,24},{12,28},{16,0},{20,4},{24,8},{28,12},{1,17},{... | collective-permute-start | bytes 12582920 | tf_op jit(solution)/shard_map/ppermute | solution.py:12
  234.8 6.7 %copy-start.4 = (s32[8]{0:T(128)S(1)}, s32[8]{0:T(128)}, u32[]{:S(2)}) copy-start(s32[8]{0:T(128)} %param.8) | copy-start | bytes 100
  234.8 6.9 %copy-start.1 = (f32[64]{0:T(128)S(1)}, f32[64]{0:T(128)}, u32[]{:S(2)}) copy-start(f32[64]{0:T(128)} %param.7) | copy-start | bytes 772
  234.8 6.9 %copy-start.3 = (f32[4]{0:T(128)S(1)}, f32[4]{0:T(128)}, u32[]{:S(2)}) copy-start(f32[4]{0:T(128)} %param.9) | copy-start | bytes 52
  237.8 49.5 %collective-permute-start.3 = (f32[32,4,64,128]{3,2,0,1:T(8,128)}, f32[32,4,64,128]{3,2,0,1:T(8,128)}, u32[]{:S(2)}, u32[]{:S(2)}) collective-permute-start(f32[32,4,64,128]{3,2,0,1:T(8,128)} %broadcast_select_fusion.2), channel_id=1, source_target_pairs={{0,4},{4,8},{8,12},{12,16},{16,20},{20,24},{24,28},{28,0},{1,5},{5... | collective-permute-start | bytes 12582920 | tf_op jit(solution)/shard_map/ppermute | solution.py:12
  328.6 23.4 %collective-permute-start.4 = (f32[32,64,128]{2,1,0:T(8,128)S(1)}, f32[32,64,128]{2,1,0:T(8,128)S(1)}, u32[]{:S(2)}, u32[]{:S(2)}) collective-permute-start(f32[32,64,128]{2,1,0:T(8,128)S(1)} %get-tuple-element.7), channel_id=1, source_target_pairs={{0,1},{1,2},{2,3},{4,5},{5,6},{6,7},{8,9},{9,10},{10,11},{12,13},{... | collective-permute-start | bytes 3145736 | tf_op jit(solution)/shard_map/ppermute | solution.py:18
  352.2 23.3 %collective-permute-start.5 = (f32[32,64,128]{2,1,0:T(8,128)S(1)}, f32[32,64,128]{2,1,0:T(8,128)S(1)}, u32[]{:S(2)}, u32[]{:S(2)}) collective-permute-start(f32[32,64,128]{2,1,0:T(8,128)S(1)} %multiply_add_fusion.1), channel_id=1, source_target_pairs={{0,1},{1,2},{2,3},{4,5},{5,6},{6,7},{8,9},{9,10},{10,11},{12,13},{... | collective-permute-start | bytes 3145736 | tf_op jit(solution)/shard_map/ppermute | solution.py:18
  375.7 22.4 %collective-permute-start.6 = (f32[32,64,128]{2,1,0:T(8,128)S(1)}, f32[32,64,128]{2,1,0:T(8,128)S(1)}, u32[]{:S(2)}, u32[]{:S(2)}) collective-permute-start(f32[32,64,128]{2,1,0:T(8,128)S(1)} %multiply_add_fusion), channel_id=1, source_target_pairs={{0,1},{1,2},{2,3},{4,5},{5,6},{6,7},{8,9},{9,10},{10,11},{12,13},{... | collective-permute-start | bytes 3145736 | tf_op jit(solution)/shard_map/ppermute | solution.py:18
where the time goes:
time: 408 us; the launch traced here: 401 us
  waiting for transfers between devices  324 us (79%)
  other arithmetic  43.9 us (11%)
  starting transfers between devices  19.8 us (5%)
  local copies, waits for them, and re-layouts  13 us (3%)
    ppermute x4, waiting for transfers between devices, passed_along(): return lax.ppermute(value, axis, pairs)  267 us
    ppermute x3, waiting for transfers between devices, from_behind(): return lax.ppermute(value, axis, pairs)  57.5 us
    select_n x7, other arithmetic, roll_rows(): field = jnp.where(chosen, jnp.roll(field, 1 << bit, axis=-1), field)  24.1 us
    ppermute x3, starting transfers between devices, from_behind(): return lax.ppermute(value, axis, pairs)  11.6 us
    slice x7, local copies, waits for them, and re-layouts, roll_rows(): field = jnp.where(chosen, jnp.roll(field, 1 << bit, axis=-1), field)  10.2 us
    ppermute x4, starting transfers between devices, passed_along(): return lax.ppermute(value, axis, pairs)  8.18 us
  transfers between devices with their start and end apart: 7, of which 7 were waited for; matrix products, arithmetic and copies ran while one was open for 1% of the time, Pallas kernels for 0%

commit v1 on v0

v1 whole, which is shorter than its diff:
```python
import functools

import jax
import jax.numpy as jnp
from jax import lax
from jax.experimental import pallas as pl
from jax.experimental.pallas import tpu as pltpu
from jax.sharding import PartitionSpec as P

GROUPS = 4
SUB = 8
PIECES = 8


def exchange_kernel(
    n, depth, x_ref, coef_ref, row_ref, share_ref, out_ref,
    recv, obuf, zin, s1, r1, s2, r2, own1, own2, zs, zr,
):
    tracers, levels, lats, width = x_ref.shape
    mine = tracers // n
    halves = max(1, min(PIECES // mine, lats // SUB))
    rows_of = lats // halves
    me = lax.axis_index("lon")
    lev = lax.axis_index("lev")

    def at(c):
        return c // halves, pl.ds(pl.multiple_of((c % halves) * rows_of, SUB), rows_of)

    def peer(k):
        return lax.rem(me + k, n)

    def outward(c, k):
        tt, rows = at(c)
        return pltpu.make_async_remote_copy(
            src_ref=x_ref.at[peer(k) * mine + tt, :, rows, :],
            dst_ref=recv.at[me, tt, :, rows, :],
            send_sem=s1.at[c, k], recv_sem=r1.at[c, k],
            device_id={"lon": peer(k)}, device_id_type=pl.DeviceIdType.MESH,
        )

    def homeward(c, k):
        tt, rows = at(c)
        return pltpu.make_async_remote_copy(
            src_ref=obuf.at[peer(k), tt, :, rows, :],
            dst_ref=out_ref.at[me * mine + tt, :, rows, :],
            send_sem=s2.at[c, k], recv_sem=r2.at[c, k],
            device_id={"lon": peer(k)}, device_id_type=pl.DeviceIdType.MESH,
        )

    def downward(c):
        tt, rows = at(c)
        return pltpu.make_async_remote_copy(
            src_ref=obuf.at[:, tt, levels - 1, rows, :],
            dst_ref=zin.at[:, tt, rows, :],
            send_sem=zs.at[c], recv_sem=zr.at[c],
            device_id={"lev": lax.rem(lev + 1, depth)}, device_id_type=pl.DeviceIdType.MESH,
        )

    def own_in(c):
        tt, rows = at(c)
        return pltpu.make_async_copy(
            x_ref.at[me * mine + tt, :, rows, :], recv.at[me, tt, :, rows, :], own1.at[c])

    def own_out(c):
        tt, rows = at(c)
        return pltpu.make_async_copy(
            obuf.at[me, tt, :, rows, :], out_ref.at[me * mine + tt, :, rows, :], own2.at[c])

    barrier = pltpu.get_barrier_semaphore()
    for k in range(1, n):
        pl.semaphore_signal(barrier, inc=1, device_id={"lon": peer(k)},
                            device_id_type=pl.DeviceIdType.MESH)
    for k in (1, depth - 1):
        pl.semaphore_signal(barrier, inc=1, device_id={"lev": lax.rem(lev + k, depth)},
                            device_id_type=pl.DeviceIdType.MESH)
    pl.semaphore_wait(barrier, n + 1)

    count = mine * halves

    @pl.loop(0, count)
    def _(c):
        own_in(c).start()

        @pl.loop(1, n)
        def _(k):
            outward(c, k).start()

    lane = lax.broadcasted_iota(jnp.int32, (SUB, width), 1)

    def behind(value, by):
        by %= n
        if by == 0:
            return value
        return jnp.concatenate([value[n - by:], value[:n - by]], axis=0)

    @pl.loop(0, count)
    def _(c):
        tt = c // halves
        base = (c % halves) * rows_of
        tracer = me * mine + tt
        own_in(c).wait()

        @pl.loop(1, n)
        def _(k):
            outward(c, k).wait_recv()

        @pl.loop(0, rows_of // SUB)
        def _(g):
            rows = pl.ds(pl.multiple_of(base + g * SUB, SUB), SUB)
            remainder = row_ref[0, rows, :]
            quotient = row_ref[1, rows, :]
            share = share_ref[rows, :]
            fine = [(remainder & (1 << b)) != 0 for b in range((width - 1).bit_length())]
            coarse = [(quotient & (1 << b)) != 0 for b in range((n - 1).bit_length())]
            same_block = lane >= remainder
            first_lane = lane == 0
            value = None
            for level in range(levels):
                field = recv[:, tt, level, rows, :]
                turned = pltpu.roll(field, 1, axis=2)
                left = jnp.where(first_lane[None], behind(turned, 1), turned)
                field = (1.0 - share)[None] * field + share[None] * left
                for b, chosen in enumerate(fine):
                    field = jnp.where(chosen[None], pltpu.roll(field, 1 << b, axis=2), field)
                field = jnp.where(same_block[None], field, behind(field, 1))
                for b, chosen in enumerate(coarse):
                    field = jnp.where(chosen[None], behind(field, 1 << b), field)
                field = coef_ref[0, tracer * levels + level] * field
                value = field if value is None else field + coef_ref[1, tracer * levels + level] * value
                obuf[:, tt, level, rows, :] = value

        def add_above(level):
            @pl.loop(0, rows_of // SUB)
            def _(g):
                rows = pl.ds(pl.multiple_of(base + g * SUB, SUB), SUB)
                obuf[:, tt, level, rows, :] += (
                    coef_ref[2, tracer * levels + level] * zin[:, tt, rows, :])

        @pl.when(lev > 0)
        def _():
            downward(c).wait_recv()
            add_above(levels - 1)

        @pl.when(lev < depth - 1)
        def _():
            downward(c).start()

        @pl.when(lev > 0)
        def _():
            for level in range(levels - 1):
                add_above(level)

        own_out(c).start()

        @pl.loop(1, n)
        def _(k):
            homeward(c, k).start()

    @pl.loop(0, count)
    def _(c):
        own_out(c).wait()

        @pl.when(lev < depth - 1)
        def _():
            downward(c).wait_send()

        @pl.loop(1, n)
        def _(k):
            outward(c, k).wait_send()
            homeward(c, k).wait()


def on_device(tracers, offsets, fraction, bin_class, thickness):
    count, levels, lats, width = tracers.shape
    n = lax.axis_size("lon")
    depth = lax.axis_size("lev")
    mine = count // n
    pieces = mine * max(1, min(PIECES // mine, lats // SUB))
    speed = 0.5 * jnp.exp2(jnp.repeat(bin_class, GROUPS).astype(jnp.float32))
    ratio = speed[:, None] / thickness[None, :]
    keep = 1.0 / (1.0 + ratio)
    carry = ratio * keep
    reach = [carry[:, 0]]
    for level in range(1, levels):
        reach.append(reach[-1] * carry[:, level])
    coef = jnp.stack([keep, carry, jnp.stack(reach, axis=1)]).reshape(3, count * levels)
    row = jnp.broadcast_to(
        jnp.stack([offsets % width, offsets // width])[:, :, None], (2, lats, width))
    share = jnp.broadcast_to(fraction[:, None], (lats, width))
    hbm = pl.BlockSpec(memory_space=pl.ANY)
    vmem = pl.BlockSpec(memory_space=pltpu.VMEM)
    sem = pltpu.SemaphoreType.DMA
    return pl.pallas_call(
        functools.partial(exchange_kernel, n, depth),
        out_shape=jax.ShapeDtypeStruct(tracers.shape, jnp.float32),
        in_specs=[hbm, pl.BlockSpec(memory_space=pltpu.SMEM), vmem, vmem],
        out_specs=hbm,
        scratch_shapes=[
            pltpu.VMEM((n, mine, levels, lats, width), jnp.float32),
            pltpu.VMEM((n, mine, levels, lats, width), jnp.float32),
            pltpu.VMEM((n, mine, lats, width), jnp.float32),
            sem((pieces, n)), sem((pieces, n)), sem((pieces, n)), sem((pieces, n)),
            sem((pieces,)), sem((pieces,)), sem((pieces,)), sem((pieces,)),
        ],
        compiler_params=pltpu.CompilerParams(
            collective_id=0, has_side_effects=True, vmem_limit_bytes=24 << 20),
    )(tracers, coef, row, share)


def solution(mesh):
    in_specs = (P(None, "lev", None, "lon"), P(), P(), P(), P("lev"))
    out_specs = P(None, "lev", None, "lon")
    return jax.shard_map(
        on_device, mesh=mesh, in_specs=in_specs, out_specs=out_specs, check_vma=False
    )
```

time: 408 us -> 108 us (0.26); the launches traced: 401 us -> 108 us
  waiting for transfers between devices: 324 us -> 0 us
  Pallas kernels: 0 us -> 99.5 us
  other arithmetic: 43.9 us -> 2.11 us
  starting transfers between devices: 19.8 us -> 0 us
  local copies, waits for them, and re-layouts: 13 us -> 6.3 us
    ppermute x7 -> x0, waiting for transfers between devices: 324 us -> none  [the longest x4 267 us: passed_along(): return lax.ppermute(value, axis, pairs)]
    pallas_call x0 -> x1, Pallas kernels: none -> 99.5 us  [on_device(): pl.pallas_call(functools.partial(exchange_kernel, n, depth), out_shape=ja...]
    select_n x10 -> x0, other arithmetic: 29.9 us -> none  [the longest x7 24.1 us: roll_rows(): field = jnp.where(chosen, jnp.roll(field, 1 << bit, axis=-1), field)]
    ppermute x7 -> x0, starting transfers between devices: 19.8 us -> none  [the longest x3 11.6 us: from_behind(): return lax.ppermute(value, axis, pairs)]
    slice x7 -> x0, local copies, waits for them, and re-layouts: 10.2 us -> none  [roll_rows(): field = jnp.where(chosen, jnp.roll(field, 1 << bit, axis=-1), field)]
    add x4 -> x0, other arithmetic: 6.82 us -> none  [the longest x1 5.83 us: on_device(): moved = (1.0 - share) * left_part + share * right_part]
  transfers between devices with their start and end apart: 7 -> 0, of which waited for: 7 -> 0; matrix products, arithmetic and copies ran while one was open for 1% -> 0% of each run, Pallas kernels for 0% -> 0%
where the time goes in v1:
time: 108 us
  Pallas kernels  99.5 us (92%)
  local copies, waits for them, and re-layouts  6.3 us (6%)
  other arithmetic  2.11 us (2%)
    pallas_call x1, Pallas kernels, on_device(): pl.pallas_call(functools.partial(exchange_kernel, n, depth), out_shape=ja...  99.5 us
    unnamed x3, local copies, waits for them, and re-layouts  4.21 us

profile of v1, /device:TPU:1, one launch (start us, length us, event | category | flops | bytes accessed | tf_op | source)
XLA Modules:
  0.0 108.0 jit_solution(17461323993390315933)
XLA Ops:
  0.0 0.7 exponential_multiply_fusion
  0.7 0.7 fusion
  1.3 0.1 broadcast_in_dim.6
  1.4 0.1 mul.44
  1.5 0.7 divide_multiply_fusion
  2.3 0.1 copy.7
  2.3 0.1 stack.24
  2.5 0.1 div.64
  2.5 0.1 div.65
  2.6 0.7 div.66.clone
  3.3 0.1 div.67
  3.4 0.7 broadcast_in_dim.8.share_ref
  4.2 0.1 broadcast_in_dim.7.row_ref
  4.2 0.0 copy-start
  4.3 2.2 %copy-done = f32[32,4,64,128]{3,2,1,0:T(8,128)S(1)} copy-done((f32[32,4,64,128]{3,2,1,0:T(8,128)S(1)}, f32[32,4,64,128]{3,2,1,0:T(8,128)}, u32[]{:S(2)}) %copy-start) | copy-done | bytes 4194328
  6.4 99.5 %shard_map.55 = f32[32,4,64,128]{3,2,1,0:T(8,128)S(1)} custom-call(f32[32,4,64,128]{3,2,1,0:T(8,128)S(1)} %copy-done, f32[3,128]{1,0:T(4,128)S(1)} %pad_maximum_fusion.1.coef_ref, s32[2,64,128]{2,1,0:T(8,128)S(1)} %broadcast_in_dim.7.row_ref, f32[64,128]{1,0:T(8,128)S(1)} %broadcast_in_dim.8.share_ref), custom_call_target="tpu_custom_call" | custom-call | tf_op jit(solution)/shard_map/pallas_call | solution.py:193
  106.0 2.0 %copy.9 = f32[32,4,64,128]{3,2,1,0:T(8,128)} copy(f32[32,4,64,128]{3,2,1,0:T(8,128)S(1)} %shard_map.55) | data formatting | bytes 8388608
  (5 shorter events, 0.1 us)
Async XLA Ops:
  4.2 2.2 %copy-start = (f32[32,4,64,128]{3,2,1,0:T(8,128)S(1)}, f32[32,4,64,128]{3,2,1,0:T(8,128)}, u32[]{:S(2)}) copy-start(f32[32,4,64,128]{3,2,1,0:T(8,128)} %x_ref.1) | copy-start | bytes 12582916

commit v2 on v1

--- a/solution.py
+++ b/solution.py
@@ -10,11 +10,12 @@
 GROUPS = 4
 SUB = 8
 PIECES = 8
+HOLD = 5
 
 
 def exchange_kernel(
-    n, depth, x_ref, coef_ref, row_ref, share_ref, out_ref,
-    recv, obuf, zin, s1, r1, s2, r2, own1, own2, zs, zr,
+    n, depth, x_ref, offsets_ref, fraction_ref, class_ref, thick_ref, out_ref,
+    recv, obuf, zin, row_ref, share_ref, s1, r1, s2, r2, own1, own2, zs, zr,
 ):
     tracers, levels, lats, width = x_ref.shape
     mine = tracers // n
@@ -85,6 +86,19 @@
         def _(k):
             outward(c, k).start()
 
+    @pl.loop(0, lats)
+    def _(j):
+        shift = jnp.full((1, width), offsets_ref[j], jnp.int32)
+        row_ref[pl.ds(j, 1), :] = shift
+        share_ref[pl.ds(j, 1), :] = jnp.full((1, width), fraction_ref[j], jnp.float32)
+
+    def ratios(tracer):
+        bin_class = jnp.full((SUB, width), class_ref[tracer // GROUPS], jnp.int32)
+        speed = 0.5
+        for b in range(3):
+            speed = speed * jnp.where((bin_class & (1 << b)) != 0, 2.0 ** (1 << b), 1.0)
+        return [speed / thick_ref[level] for level in range(levels)]
+
     lane = lax.broadcasted_iota(jnp.int32, (SUB, width), 1)
 
     def behind(value, by):
@@ -93,11 +107,12 @@
             return value
         return jnp.concatenate([value[n - by:], value[:n - by]], axis=0)
 
-    @pl.loop(0, count)
-    def _(c):
+    def turn(c):
         tt = c // halves
         base = (c % halves) * rows_of
-        tracer = me * mine + tt
+        ratio = ratios(me * mine + tt)
+        keep = [1.0 / (1.0 + r) for r in ratio]
+        carry = [r * k for r, k in zip(ratio, keep)]
         own_in(c).wait()
 
         @pl.loop(1, n)
@@ -107,8 +122,9 @@
         @pl.loop(0, rows_of // SUB)
         def _(g):
             rows = pl.ds(pl.multiple_of(base + g * SUB, SUB), SUB)
-            remainder = row_ref[0, rows, :]
-            quotient = row_ref[1, rows, :]
+            shift = row_ref[rows, :]
+            remainder = lax.rem(shift, width)
+            quotient = lax.div(shift, width)
             share = share_ref[rows, :]
             fine = [(remainder & (1 << b)) != 0 for b in range((width - 1).bit_length())]
             coarse = [(quotient & (1 << b)) != 0 for b in range((n - 1).bit_length())]
@@ -125,16 +141,23 @@
                 field = jnp.where(same_block[None], field, behind(field, 1))
                 for b, chosen in enumerate(coarse):
                     field = jnp.where(chosen[None], behind(field, 1 << b), field)
-                field = coef_ref[0, tracer * levels + level] * field
-                value = field if value is None else field + coef_ref[1, tracer * levels + level] * value
+                field = keep[level][None] * field
+                value = field if value is None else field + carry[level][None] * value
                 obuf[:, tt, level, rows, :] = value
+
+    def settle(c):
+        tt = c // halves
+        base = (c % halves) * rows_of
+        reach = []
+        for r in ratios(me * mine + tt):
+            step = r / (1.0 + r)
+            reach.append(reach[-1] * step if reach else step)
 
         def add_above(level):
             @pl.loop(0, rows_of // SUB)
             def _(g):
                 rows = pl.ds(pl.multiple_of(base + g * SUB, SUB), SUB)
-                obuf[:, tt, level, rows, :] += (
-                    coef_ref[2, tracer * levels + level] * zin[:, tt, rows, :])
+                obuf[:, tt, level, rows, :] += reach[level][None] * zin[:, tt, rows, :]
 
         @pl.when(lev > 0)
         def _():
@@ -150,11 +173,38 @@
             for level in range(levels - 1):
                 add_above(level)
 
+    def send_home(c):
         own_out(c).start()
 
         @pl.loop(1, n)
         def _(k):
             homeward(c, k).start()
+
+    hold = min(HOLD, count - 1)
+
+    @pl.loop(0, count + depth - 1)
+    def _(i):
+        @pl.when(i < count)
+        def _():
+            turn(i)
+
+        done = i - lev
+
+        @pl.when((done >= 0) & (done < count))
+        def _():
+            settle(done)
+
+        @pl.when((done >= 0) & (done < count) & (i > hold))
+        def _():
+            send_home(done)
+
+        @pl.when(i == hold)
+        def _():
+            @pl.loop(0, count)
+            def _(c):
+                @pl.when(c <= done)
+                def _():
+                    send_home(c)
 
     @pl.loop(0, count)
     def _(c):
@@ -176,35 +226,25 @@
     depth = lax.axis_size("lev")
     mine = count // n
     pieces = mine * max(1, min(PIECES // mine, lats // SUB))
-    speed = 0.5 * jnp.exp2(jnp.repeat(bin_class, GROUPS).astype(jnp.float32))
-    ratio = speed[:, None] / thickness[None, :]
-    keep = 1.0 / (1.0 + ratio)
-    carry = ratio * keep
-    reach = [carry[:, 0]]
-    for level in range(1, levels):
-        reach.append(reach[-1] * carry[:, level])
-    coef = jnp.stack([keep, carry, jnp.stack(reach, axis=1)]).reshape(3, count * levels)
-    row = jnp.broadcast_to(
-        jnp.stack([offsets % width, offsets // width])[:, :, None], (2, lats, width))
-    share = jnp.broadcast_to(fraction[:, None], (lats, width))
-    hbm = pl.BlockSpec(memory_space=pl.ANY)
-    vmem = pl.BlockSpec(memory_space=pltpu.VMEM)
+    smem = pl.BlockSpec(memory_space=pltpu.SMEM)
     sem = pltpu.SemaphoreType.DMA
     return pl.pallas_call(
         functools.partial(exchange_kernel, n, depth),
         out_shape=jax.ShapeDtypeStruct(tracers.shape, jnp.float32),
-        in_specs=[hbm, pl.BlockSpec(memory_space=pltpu.SMEM), vmem, vmem],
-        out_specs=hbm,
+        in_specs=[pl.BlockSpec(memory_space=pltpu.HBM), smem, smem, smem, smem],
+        out_specs=pl.BlockSpec(memory_space=pl.ANY),
         scratch_shapes=[
             pltpu.VMEM((n, mine, levels, lats, width), jnp.float32),
             pltpu.VMEM((n, mine, levels, lats, width), jnp.float32),
             pltpu.VMEM((n, mine, lats, width), jnp.float32),
+            pltpu.VMEM((lats, width), jnp.int32),
+            pltpu.VMEM((lats, width), jnp.float32),
             sem((pieces, n)), sem((pieces, n)), sem((pieces, n)), sem((pieces, n)),
             sem((pieces,)), sem((pieces,)), sem((pieces,)), sem((pieces,)),
         ],
         compiler_params=pltpu.CompilerParams(
-            collective_id=0, has_side_effects=True, vmem_limit_bytes=24 << 20),
-    )(tracers, coef, row, share)
+            collective_id=0, has_side_effects=True, vmem_limit_bytes=58 << 20),
+    )(tracers, offsets, fraction, bin_class, thickness)
 
 
 def solution(mesh):

time: 108 us -> 105 us (0.972)
  other arithmetic: 2.11 us -> 0 us
  local copies, waits for them, and re-layouts: 6.3 us -> 4.79 us
    mul x4 -> x0, other arithmetic: 1.41 us -> none  [the longest x2 0.74 us: on_device(): carry = ratio * keep]
    unnamed x3 -> x1, local copies, waits for them, and re-layouts: 4.21 us -> 4.79 us
where the time goes in v2:
time: 105 us
  Pallas kernels  99.9 us (95%)
  local copies, waits for them, and re-layouts  4.79 us (5%)
    pallas_call x1, Pallas kernels, on_device(): pl.pallas_call(functools.partial(exchange_kernel, n, depth), out_shape=ja...  99.9 us
    unnamed x1, local copies, waits for them, and re-layouts  4.79 us

profile of v2, /device:TPU:1, one launch (start us, length us, event | category | flops | bytes accessed | tf_op | source)
XLA Modules:
  0.0 104.7 jit_solution(13583582279698463170)
XLA Ops:
  0.0 99.9 %shard_map.55 = f32[32,4,64,128]{3,2,1,0:T(8,128)} custom-call(f32[32,4,64,128]{3,2,1,0:T(8,128)} %x_ref.1, s32[64]{0:T(128)} %offsets_ref.1, f32[64]{0:T(128)} %fraction_ref.1, s32[8]{0:T(128)} %class_ref.1, f32[4]{0:T(128)} %thick_ref.1), custom_call_target="tpu_custom_call" | custom-call | tf_op jit(solution)/shard_map/pallas_call | solution.py:231
  99.9 4.8 %copy.7 = f32[32,4,64,128]{3,2,1,0:T(8,128)} copy(f32[32,4,64,128]{3,2,1,0:T(8,128)} %shard_map.55) | data formatting | bytes 8388608

commit v3 on v2

--- a/solution.py
+++ b/solution.py
@@ -14,8 +14,8 @@
 
 
 def exchange_kernel(
-    n, depth, x_ref, offsets_ref, fraction_ref, class_ref, thick_ref, out_ref,
-    recv, obuf, zin, row_ref, share_ref, s1, r1, s2, r2, own1, own2, zs, zr,
+    n, depth, x_ref, offsets_hbm, fraction_hbm, class_hbm, thick_hbm, out_ref,
+    offsets_ref, fraction_ref, class_ref, thick_ref, small, recv, obuf, zin, row_ref, share_ref, s1, r1, s2, r2, own1, own2, zs, zr,
 ):
     tracers, levels, lats, width = x_ref.shape
     mine = tracers // n
@@ -66,6 +66,15 @@
         tt, rows = at(c)
         return pltpu.make_async_copy(
             obuf.at[me, tt, :, rows, :], out_ref.at[me * mine + tt, :, rows, :], own2.at[c])
+
+    scalars = [
+        pltpu.make_async_copy(source, held, small.at[i])
+        for i, (source, held) in enumerate((
+            (offsets_hbm, offsets_ref), (fraction_hbm, fraction_ref),
+            (class_hbm, class_ref), (thick_hbm, thick_ref)))
+    ]
+    for copy in scalars:
+        copy.start()
 
     barrier = pltpu.get_barrier_semaphore()
     for k in range(1, n):
@@ -85,6 +94,9 @@
         @pl.loop(1, n)
         def _(k):
             outward(c, k).start()
+
+    for copy in scalars:
+        copy.wait()
 
     @pl.loop(0, lats)
     def _(j):
@@ -226,14 +238,16 @@
     depth = lax.axis_size("lev")
     mine = count // n
     pieces = mine * max(1, min(PIECES // mine, lats // SUB))
-    smem = pl.BlockSpec(memory_space=pltpu.SMEM)
+    hbm = pl.BlockSpec(memory_space=pltpu.HBM)
+    held = [pltpu.SMEM(a.shape, a.dtype) for a in (offsets, fraction, bin_class, thickness)]
     sem = pltpu.SemaphoreType.DMA
     return pl.pallas_call(
         functools.partial(exchange_kernel, n, depth),
         out_shape=jax.ShapeDtypeStruct(tracers.shape, jnp.float32),
-        in_specs=[pl.BlockSpec(memory_space=pltpu.HBM), smem, smem, smem, smem],
+        in_specs=[hbm] * 5,
         out_specs=pl.BlockSpec(memory_space=pl.ANY),
         scratch_shapes=[
+            *held, sem((4,)),
             pltpu.VMEM((n, mine, levels, lats, width), jnp.float32),
             pltpu.VMEM((n, mine, levels, lats, width), jnp.float32),
             pltpu.VMEM((n, mine, lats, width), jnp.float32),
@@ -243,8 +257,9 @@
             sem((pieces,)), sem((pieces,)), sem((pieces,)), sem((pieces,)),
         ],
         compiler_params=pltpu.CompilerParams(
-            collective_id=0, has_side_effects=True, vmem_limit_bytes=58 << 20),
-    )(tracers, offsets, fraction, bin_class, thickness)
+            collective_id=0, has_side_effects=True, vmem_limit_bytes=24 << 20),
+    )(*(pltpu.with_memory_space_constraint(a, pltpu.HBM)
+        for a in (tracers, offsets, fraction, bin_class, thickness)))
 
 
 def solution(mesh):

time: 105 us -> 101 us (0.962)
  local copies, waits for them, and re-layouts: 4.79 us -> 2.02 us
    unnamed x1, local copies, waits for them, and re-layouts: 4.79 us -> 2.02 us
where the time goes in v3:
time: 101 us
  Pallas kernels  99.1 us (98%)
  local copies, waits for them, and re-layouts  2.02 us (2%)
    pallas_call x1, Pallas kernels, on_device(): pl.pallas_call(functools.partial(exchange_kernel, n, depth), out_shape=ja...  99.1 us

profile of v3, /device:TPU:1, one launch (start us, length us, event | category | flops | bytes accessed | tf_op | source)
XLA Modules:
  0.0 101.1 jit_solution(6702223886973848725)
XLA Ops:
  0.0 99.1 %shard_map.55 = f32[32,4,64,128]{3,2,1,0:T(8,128)S(1)} custom-call(f32[32,4,64,128]{3,2,1,0:T(8,128)} %x_ref.1, s32[64]{0:T(128)} %offsets_hbm.1, f32[64]{0:T(128)} %fraction_hbm.1, s32[8]{0:T(128)} %class_hbm.1, f32[4]{0:T(128)} %thick_hbm.1), custom_call_target="tpu_custom_call" | custom-call | tf_op jit(solution)/shard_map/pallas_call | solution.py:244
  99.1 2.0 %copy.7 = f32[32,4,64,128]{3,2,1,0:T(8,128)} copy(f32[32,4,64,128]{3,2,1,0:T(8,128)S(1)} %shard_map.55) | data formatting | bytes 8388608

commit v4 on v3

--- a/solution.py
+++ b/solution.py
@@ -10,7 +10,7 @@
 GROUPS = 4
 SUB = 8
 PIECES = 8
-HOLD = 5
+HOLD = 3
 
 
 def exchange_kernel(
@@ -30,21 +30,19 @@
     def peer(k):
         return lax.rem(me + k, n)
 
-    def outward(c, k):
-        tt, rows = at(c)
+    def outward(tt, k):
         return pltpu.make_async_remote_copy(
-            src_ref=x_ref.at[peer(k) * mine + tt, :, rows, :],
-            dst_ref=recv.at[me, tt, :, rows, :],
-            send_sem=s1.at[c, k], recv_sem=r1.at[c, k],
+            src_ref=x_ref.at[peer(k) * mine + tt],
+            dst_ref=recv.at[me, tt],
+            send_sem=s1.at[tt, k], recv_sem=r1.at[tt, k],
             device_id={"lon": peer(k)}, device_id_type=pl.DeviceIdType.MESH,
         )
 
-    def homeward(c, k):
-        tt, rows = at(c)
+    def homeward(tt, k):
         return pltpu.make_async_remote_copy(
-            src_ref=obuf.at[peer(k), tt, :, rows, :],
-            dst_ref=out_ref.at[me * mine + tt, :, rows, :],
-            send_sem=s2.at[c, k], recv_sem=r2.at[c, k],
+            src_ref=obuf.at[peer(k), tt],
+            dst_ref=out_ref.at[me * mine + tt],
+            send_sem=s2.at[tt, k], recv_sem=r2.at[tt, k],
             device_id={"lon": peer(k)}, device_id_type=pl.DeviceIdType.MESH,
         )
 
@@ -57,15 +55,11 @@
             device_id={"lev": lax.rem(lev + 1, depth)}, device_id_type=pl.DeviceIdType.MESH,
         )
 
-    def own_in(c):
-        tt, rows = at(c)
-        return pltpu.make_async_copy(
-            x_ref.at[me * mine + tt, :, rows, :], recv.at[me, tt, :, rows, :], own1.at[c])
-
-    def own_out(c):
-        tt, rows = at(c)
-        return pltpu.make_async_copy(
-            obuf.at[me, tt, :, rows, :], out_ref.at[me * mine + tt, :, rows, :], own2.at[c])
+    def own_in(tt):
+        return pltpu.make_async_copy(x_ref.at[me * mine + tt], recv.at[me, tt], own1.at[tt])
+
+    def own_out(tt):
+        return pltpu.make_async_copy(obuf.at[me, tt], out_ref.at[me * mine + tt], own2.at[tt])
 
     scalars = [
         pltpu.make_async_copy(source, held, small.at[i])
@@ -87,13 +81,13 @@
 
     count = mine * halves
 
-    @pl.loop(0, count)
-    def _(c):
-        own_in(c).start()
-
+    @pl.loop(0, mine)
+    def _(tt):
         @pl.loop(1, n)
         def _(k):
-            outward(c, k).start()
+            outward(tt, k).start()
+
+        own_in(tt).start()
 
     for copy in scalars:
         copy.wait()
@@ -125,11 +119,14 @@
         ratio = ratios(me * mine + tt)
         keep = [1.0 / (1.0 + r) for r in ratio]
         carry = [r * k for r, k in zip(ratio, keep)]
-        own_in(c).wait()
-
-        @pl.loop(1, n)
-        def _(k):
-            outward(c, k).wait_recv()
+
+        @pl.when(c % halves == 0)
+        def _():
+            own_in(tt).wait()
+
+            @pl.loop(1, n)
+            def _(k):
+                outward(tt, k).wait_recv()
 
         @pl.loop(0, rows_of // SUB)
         def _(g):
@@ -185,12 +182,12 @@
             for level in range(levels - 1):
                 add_above(level)
 
-    def send_home(c):
-        own_out(c).start()
-
+    def send_home(tt):
         @pl.loop(1, n)
         def _(k):
-            homeward(c, k).start()
+            homeward(tt, k).start()
+
+        own_out(tt).start()
 
     hold = min(HOLD, count - 1)
 
@@ -206,30 +203,32 @@
         def _():
             settle(done)
 
-        @pl.when((done >= 0) & (done < count) & (i > hold))
-        def _():
-            send_home(done)
+        @pl.when((done >= 0) & (done < count) & (done % halves == halves - 1) & (i > hold))
+        def _():
+            send_home(done // halves)
 
         @pl.when(i == hold)
         def _():
-            @pl.loop(0, count)
-            def _(c):
-                @pl.when(c <= done)
+            @pl.loop(0, mine)
+            def _(tt):
+                @pl.when((tt + 1) * halves - 1 <= done)
                 def _():
-                    send_home(c)
-
-    @pl.loop(0, count)
-    def _(c):
-        own_out(c).wait()
-
-        @pl.when(lev < depth - 1)
-        def _():
+                    send_home(tt)
+
+    @pl.when(lev < depth - 1)
+    def _():
+        @pl.loop(0, count)
+        def _(c):
             downward(c).wait_send()
+
+    @pl.loop(0, mine)
+    def _(tt):
+        own_out(tt).wait()
 
         @pl.loop(1, n)
         def _(k):
-            outward(c, k).wait_send()
-            homeward(c, k).wait()
+            outward(tt, k).wait_send()
+            homeward(tt, k).wait()
 
 
 def on_device(tracers, offsets, fraction, bin_class, thickness):
@@ -253,8 +252,8 @@
             pltpu.VMEM((n, mine, lats, width), jnp.float32),
             pltpu.VMEM((lats, width), jnp.int32),
             pltpu.VMEM((lats, width), jnp.float32),
-            sem((pieces, n)), sem((pieces, n)), sem((pieces, n)), sem((pieces, n)),
-            sem((pieces,)), sem((pieces,)), sem((pieces,)), sem((pieces,)),
+            sem((mine, n)), sem((mine, n)), sem((mine, n)), sem((mine, n)),
+            sem((mine,)), sem((mine,)), sem((pieces,)), sem((pieces,)),
         ],
         compiler_params=pltpu.CompilerParams(
             collective_id=0, has_side_effects=True, vmem_limit_bytes=24 << 20),

time: 101 us -> 100 us (0.990)
  no operation moved by 1% of the time
where the time goes in v4:
time: 100 us
  Pallas kernels  98.2 us (98%)
  local copies, waits for them, and re-layouts  2.02 us (2%)
    pallas_call x1, Pallas kernels, on_device(): pl.pallas_call(functools.partial(exchange_kernel, n, depth), out_shape=ja...  98.2 us
    unnamed x1, local copies, waits for them, and re-layouts  2.02 us

profile of v4, /device:TPU:1, one launch (start us, length us, event | category | flops | bytes accessed | tf_op | source)
XLA Modules:
  0.0 100.2 jit_solution(7606631372232860992)
XLA Ops:
  0.0 98.2 %shard_map.55 = f32[32,4,64,128]{3,2,1,0:T(8,128)S(1)} custom-call(f32[32,4,64,128]{3,2,1,0:T(8,128)} %x_ref.1, s32[64]{0:T(128)} %offsets_hbm.1, f32[64]{0:T(128)} %fraction_hbm.1, s32[8]{0:T(128)} %class_hbm.1, f32[4]{0:T(128)} %thick_hbm.1), custom_call_target="tpu_custom_call" | custom-call | tf_op jit(solution)/shard_map/pallas_call | solution.py:243
  98.2 2.0 %copy.7 = f32[32,4,64,128]{3,2,1,0:T(8,128)} copy(f32[32,4,64,128]{3,2,1,0:T(8,128)S(1)} %shard_map.55) | data formatting | bytes 8388608
